TPU v7x, 32 devices: a whole 2x2x4 slice. The times are simulated.
32 devices in a mesh: segment: 2 (over core), expert: 8 (over z, y), dp: 2 (over x).
Axes of the slice: x: 2, y: 2, z: 4, core: 2. Of those that a mesh axis runs over, the one named last changes fastest.
Arguments:
- moe_input: bfloat16 [2, 1024, 2688], P('segment', 'expert', 'dp'), may hold values from -64 to 64
- norm_gain: float32 [2688], replicated, may hold values from 0.1 to 1.9
- routes: int32 [2, 1024, 6], P('segment', 'expert'), may hold values from 0 to 15, all different within a row; in each aligned block of 128 rows (0 to 127, 128 to 255, ..., all dimensions but the last counted through in order) at most 54 rows name the same one
- route_scores: float32 [2, 1024, 6], P('segment', 'expert'), may hold values from -8 to 8
- w_up: bfloat16 [16, 2688, 1856], P('expert', None, 'dp'), may hold values from -0.125 to 0.125
- w_down: bfloat16 [16, 1856, 2688], P('expert', None, 'dp'), may hold values from -0.125 to 0.125
- queries: bfloat16 [2, 1024, 2048], P('segment', 'expert', 'dp'), may hold values from -100 to 100
- keys: bfloat16 [2, 1024, 256], P('segment', 'expert'), may hold values from -6 to 6
- values: bfloat16 [2, 1024, 256], P('segment', 'expert'), may hold values from -6 to 6
- out_grad: bfloat16 [2, 1024, 2688], P('segment', 'expert'), may hold values from -6 to 6
- w_query: bfloat16 [2688, 2048], P(None, 'dp'), may hold values from -0.125 to 0.125
- w_key: bfloat16 [2688, 256], replicated, may hold values from -0.125 to 0.125
- w_value: bfloat16 [2688, 256], replicated, may hold values from -0.125 to 0.125
- w_out: bfloat16 [2048, 2688], P('dp'), may hold values from -0.125 to 0.125
Outputs:
- moe_next: bfloat16 [2, 1024, 2688], P('segment', 'expert', 'dp')
- grad_prev: bfloat16 [2, 1024, 2688], P('segment', 'expert', 'dp')
Inputs may be any that keep to these rules, and one draw needn't show every extreme that they name: `routes`: each row names 6 different experts. Among the 128 rows of one sequence no expert is named more than 54 times, a bound that some block reaches; every expert is named by some row.
All inputs are finite; a program needn't handle non-finite values.
Results may differ from a plain program's by a relative error of at most 0.028.
Values may be sent and summed in bfloat16 or wider, within the bound.
No kernel may reach another device: no remote copies, remote signals or barrier semaphores. Data moves between devices by JAX's collectives and lax.ppermute only.
A program may use at most 128 MiB of HBM per device.

v0:
```python
import jax
import jax.numpy as jnp
from jax import lax
from jax.sharding import PartitionSpec as P

D = 2688
HEADS = 16
KV_HEADS = 2
HEAD_DIM = 128
TOPK = 6
NORM_EPSILON = 1e-05


def partner(block, axis, distance):
    count = lax.axis_size(axis)
    route = []
    for low in range(count):
        high = low | 1 << distance
        if high != low and high < count:
            route += [(low, high), (high, low)]
    return lax.ppermute(block, axis, route)


def attention_grad(queries, keys, values, out_grad, w_query, w_key, w_value, w_out, block_index):
    token_count = queries.shape[0]
    query_width = queries.shape[1]
    heads_here = query_width // HEAD_DIM
    group_size = HEADS // KV_HEADS
    score_scale = HEAD_DIM ** (-0.5)
    head_group = block_index * heads_here // group_size
    kv_start = head_group * HEAD_DIM
    key_head = lax.dynamic_slice_in_dim(keys, kv_start, HEAD_DIM, 1)
    value_head = lax.dynamic_slice_in_dim(values, kv_start, HEAD_DIM, 1)
    key_weight = lax.dynamic_slice_in_dim(w_key, kv_start, HEAD_DIM, 1)
    value_weight = lax.dynamic_slice_in_dim(w_value, kv_start, HEAD_DIM, 1)
    d_attn = jnp.einsum("td,qd->tq", out_grad, w_out, preferred_element_type=jnp.float32).astype(
        jnp.bfloat16
    )
    grad_heads = d_attn.reshape(token_count, heads_here, HEAD_DIM)
    query_heads = queries.reshape(token_count, heads_here, HEAD_DIM)
    scores = (
        jnp.einsum("ihd,jd->hij", query_heads, key_head, preferred_element_type=jnp.float32)
        * score_scale
    )
    positions = jnp.arange(token_count, dtype=jnp.int32)
    causal = positions[None, :] <= positions[:, None]
    scores = jnp.where(causal[None], scores, -jnp.inf)
    peak = jnp.max(scores, axis=2, keepdims=True)
    raised = jnp.exp(scores - peak)
    attn_weights = raised / jnp.sum(raised, axis=2, keepdims=True)
    d_weights = jnp.einsum(
        "ihd,jd->hij", grad_heads, value_head, preferred_element_type=jnp.float32
    )
    row_delta = jnp.sum(attn_weights * d_weights, axis=2, keepdims=True)
    d_scores = (attn_weights * (d_weights - row_delta)).astype(jnp.bfloat16)
    d_query = (
        jnp.einsum("hij,jd->ihd", d_scores, key_head, preferred_element_type=jnp.float32)
        * score_scale
    )
    d_query = d_query.astype(jnp.bfloat16).reshape(token_count, query_width)
    d_key = (
        jnp.einsum("hij,ihd->jd", d_scores, query_heads, preferred_element_type=jnp.float32)
        * score_scale
    ).astype(jnp.bfloat16)
    d_value = jnp.einsum(
        "hij,ihd->jd",
        attn_weights.astype(jnp.bfloat16),
        grad_heads,
        preferred_element_type=jnp.float32,
    ).astype(jnp.bfloat16)
    grad_term = jnp.einsum("tq,dq->td", d_query, w_query, preferred_element_type=jnp.float32)
    grad_term = grad_term + jnp.einsum(
        "tk,dk->td", d_key, key_weight, preferred_element_type=jnp.float32
    )
    grad_term = grad_term + jnp.einsum(
        "tk,dk->td", d_value, value_weight, preferred_element_type=jnp.float32
    )
    return grad_term


def block_product(block_rows, w_up, first_feature):
    width = block_rows.shape[3]
    weight_rows = lax.dynamic_slice_in_dim(w_up, first_feature, width, 1)
    product = jnp.einsum(
        "sjcw,jwh->sjch", block_rows, weight_rows, preferred_element_type=jnp.float32
    )
    return lax.optimization_barrier(product.astype(jnp.bfloat16)).astype(jnp.float32)


def on_device(
    moe_input,
    norm_gain,
    routes,
    route_scores,
    w_up,
    w_down,
    queries,
    keys,
    values,
    out_grad,
    w_query,
    w_key,
    w_value,
    w_out,
):
    columns = lax.axis_size("expert")
    token_count = moe_input.shape[1]
    feature_share = moe_input.shape[2]
    local_experts = w_up.shape[0]
    hidden_share = w_up.shape[2]
    expert_count = local_experts * columns
    capacity = (9 * token_count * TOPK + 8 * expert_count - 1) // (8 * expert_count)
    slot_count = expert_count * capacity
    feature_index = lax.axis_index("dp")
    token_rows = moe_input[0]
    chosen_experts = routes[0]
    logits = route_scores[0]
    flat_choices = chosen_experts.reshape(-1)
    expert_hits = (
        flat_choices[:, None] == jnp.arange(expert_count, dtype=jnp.int32)[None, :]
    ).astype(jnp.int32)
    earlier = jnp.cumsum(expert_hits, axis=0) - expert_hits
    places = jnp.sum(earlier * expert_hits, axis=1).reshape(token_count, TOPK)
    targets = chosen_experts * capacity + places
    slot_ids = jnp.arange(slot_count, dtype=jnp.int32)
    signal = jax.nn.sigmoid(logits)
    gate_values = (
        (signal / jnp.sum(signal, axis=1, keepdims=True)).astype(jnp.bfloat16).astype(jnp.float32)
    )
    spread_sum = jnp.zeros((token_count, slot_count), jnp.float32)
    mixing_sum = jnp.zeros((token_count, slot_count), jnp.float32)
    for choice_index in range(TOPK):
        hit = slot_ids[None, :] == targets[:, choice_index : choice_index + 1]
        spread_sum = spread_sum + hit.astype(jnp.float32)
        mixing_sum = mixing_sum + jnp.where(
            hit, gate_values[:, choice_index : choice_index + 1], 0.0
        )
    spread = spread_sum.astype(jnp.bfloat16)
    mixing = mixing_sum.astype(jnp.bfloat16)
    outgoing = jnp.einsum(
        "ts,tw->sw", spread, token_rows, preferred_element_type=jnp.float32
    ).astype(jnp.bfloat16)
    outgoing = outgoing.reshape(columns, local_experts, capacity, feature_share)
    arrived = lax.all_to_all(outgoing, "expert", split_axis=0, concat_axis=0, tiled=True)
    arrived_wide = arrived.astype(jnp.float32)
    start_up = jnp.zeros((columns, local_experts, capacity, hidden_share), jnp.float32)
    squares = lax.psum(jnp.sum(jnp.square(arrived_wide), axis=3), "dp")
    gain_part = lax.dynamic_slice_in_dim(norm_gain, feature_index * feature_share, feature_share, 0)
    scaled = (arrived_wide * gain_part).astype(jnp.bfloat16)
    running = start_up
    piece = lax.all_gather(scaled, "dp", axis=3, tiled=True)
    start = jnp.int32(0)
    for block_number in range(piece.shape[3] // feature_share):
        first = block_number * feature_share
        running = running + block_product(
            piece[:, :, :, first : first + feature_share], w_up, start + first
        )
    inverse = 1.0 / jnp.sqrt(squares / D + NORM_EPSILON)
    projected = running * inverse[..., None]
    hidden = jnp.square(jnp.maximum(projected, 0.0)).astype(jnp.bfloat16)
    grad_term = attention_grad(
        queries[0], keys[0], values[0], out_grad[0], w_query, w_key, w_value, w_out, feature_index
    )
    grad_here = lax.psum_scatter(
        grad_term.astype(jnp.bfloat16), "dp", scatter_dimension=1, tiled=True
    )
    expert_out = jnp.einsum(
        "sjch,jhd->sjcd",
        lax.all_gather(hidden, "dp", axis=3, tiled=True),
        w_down,
        preferred_element_type=jnp.float32,
    )
    expert_rows = expert_out.astype(jnp.bfloat16)
    returned = lax.all_to_all(expert_rows, "expert", split_axis=0, concat_axis=0, tiled=True)
    moe_out = jnp.dot(
        mixing, returned.reshape(slot_count, feature_share), preferred_element_type=jnp.float32
    ).astype(jnp.bfloat16)
    moe_next, grad_prev = partner((moe_out, grad_here), "segment", 0)
    return (moe_next[None], grad_prev[None])


def solution(mesh):
    return jax.shard_map(
        on_device,
        mesh=mesh,
        in_specs=(
            P("segment", "expert", "dp"),
            P(),
            P("segment", "expert", None),
            P("segment", "expert", None),
            P("expert", None, "dp"),
            P("expert", None, "dp"),
            P("segment", "expert", "dp"),
            P("segment", "expert", None),
            P("segment", "expert", None),
            P("segment", "expert", None),
            P(None, "dp"),
            P(),
            P(),
            P("dp", None),
        ),
        out_specs=(P("segment", "expert", "dp"), P("segment", "expert", "dp")),
        check_vma=False,
    )
```

profile of v0, /device:TPU:0, one launch (start us, length us, event | category | flops | bytes accessed | tf_op | source)
XLA Modules:
  0.0 497.4 jit_solution(2547123518346177844)
XLA Ops:
  7.2 0.9 copy.82
  8.4 1.7 reduce-window.6
  11.5 3.5 convolution_convert_fusion
  15.0 21.9 %reshape.76 = bf16[8,2,54,1344]{2,1,0,3:T(2,128)(2,1)} reshape(bf16[864,1344]{0,1:T(8,128)(2,1)} %convolution_convert_fusion) | data formatting | bytes 4644864 | tf_op jit(solution)/shard_map/reshape | solution.py:143
  36.8 15.1 %copy.87 = bf16[8,2,54,1344]{3,1,2,0:T(2,128)(2,1)} copy(bf16[8,2,54,1344]{2,1,0,3:T(2,128)(2,1)} %reshape.76) | data formatting | bytes 4644864 | tf_op jit(solution)/shard_map/reshape | solution.py:143
  52.0 7.4 %all-to-all-start = ((bf16[8,2,54,1344]{3,1,2,0:T(2,128)(2,1)}), bf16[8,2,54,1344]{3,1,2,0:T(2,128)(2,1)}, u32[]{:S(2)}, u32[]{:S(2)}) async-start(bf16[8,2,54,1344]{3,1,2,0:T(2,128)(2,1)} %copy.87), calls=%async_computation | async-start | bytes 4866048 | tf_op jit(solution)/shard_map/all_to_all | solution.py:144
  59.5 55.4 %all-to-all-done = bf16[8,2,54,1344]{3,1,2,0:T(2,128)(2,1)} async-done(((bf16[8,2,54,1344]{3,1,2,0:T(2,128)(2,1)}), bf16[8,2,54,1344]{3,1,2,0:T(2,128)(2,1)}, u32[]{:S(2)}, u32[]{:S(2)}) %all-to-all-start) | async-done | bytes 2322464 | tf_op jit(solution)/shard_map/all_to_all | solution.py:144
  114.9 3.9 fusion.13
  118.8 8.9 %copy.89 = bf16[8,2,54,1344]{2,0,1,3:T(8,128)(2,1)} copy(bf16[8,2,54,1344]{3,0,2,1:T(8,128)(2,1)} %get-tuple-element.11) | data formatting | bytes 4644864 | tf_op jit(solution)/shard_map/convert_element_type | solution.py:149
  127.9 5.0 psum.7
  132.9 129.3 %all-gather.3.cloned.1.call-done = bf16[8,2,54,2688]{2,0,1,3:T(8,128)(2,1)} async-done(((bf16[8,2,54,1344]{2,0,1,3:T(8,128)(2,1)}), bf16[8,2,54,2688]{2,0,1,3:T(8,128)(2,1)}) %all-gather.3.cloned.1.call-update) | async-done | bytes 4644880 | tf_op jit(solution)/shard_map/all_gather | solution.py:151
  262.2 5.5 %fusion.112 = (bf16[8,2,54,1344]{2,0,1,3:T(8,128)(2,1)S(1)}, bf16[8,2,54,1344]{2,0,1,3:T(8,128)(2,1)S(1)}) fusion(bf16[8,2,54,2688]{2,0,1,3:T(8,128)(2,1)} %all-gather.3.cloned.1.call-done), kind=kLoop, calls=%fused_computation.132 | loop fusion | bytes 9289728 | tf_op jit(solution)/shard_map/slice | solution.py:156
  267.7 11.1 %convert_bitcast_fusion.1 = bf16[8,2,54,928]{3,2,0,1:T(8,128)(2,1)} fusion(bf16[2,2688,928]{1,2,0:T(8,128)(2,1)} %param.18, bf16[8,2,54,1344]{2,0,1,3:T(8,128)(2,1)S(1)} %get-tuple-element.8), kind=kOutput, calls=%fused_computation.25 | convolution fusion | flops 2156018688 | bytes 9152512 | tf_op jit(solution)/shard_map/sjcw,jwh->sjch/dot_general | solution.py:84
  278.9 10.0 %convert_bitcast_fusion = bf16[8,2,54,928]{3,2,0,1:T(8,128)(2,1)S(1)} fusion(bf16[2,2688,928]{1,2,0:T(8,128)(2,1)} %param.18, bf16[8,2,54,1344]{2,0,1,3:T(8,128)(2,1)S(1)} %get-tuple-element.9), kind=kOutput, calls=%fused_computation.24 | convolution fusion | flops 2156018688 | bytes 9152512 | tf_op jit(solution)/shard_map/sjcw,jwh->sjch/dot_general | solution.py:84
  288.9 0.8 multiply_convert_fusion
  289.7 4.9 copy.94
  294.7 95.3 %all-gather.5.cloned.1.call-done = bf16[8,2,54,1856]{2,0,1,3:T(8,128)(2,1)} async-done(((bf16[8,2,54,928]{2,0,1,3:T(8,128)(2,1)}), bf16[8,2,54,1856]{2,0,1,3:T(8,128)(2,1)}) %all-gather.5.cloned.1.call-update) | async-done | bytes 3207184 | tf_op jit(solution)/shard_map/all_gather | solution.py:169
  389.9 20.2 %fusion.20 = bf16[8,2,54,1344]{3,2,0,1:T(8,128)(2,1)} fusion(bf16[2,1856,1344]{1,2,0:T(8,128)(2,1)} %param.19, bf16[8,2,54,1856]{2,0,1,3:T(8,128)(2,1)} %all-gather.5.cloned.1.call-done), kind=kOutput, calls=%fused_computation.22 | convolution fusion | flops 4311595008 | bytes 15507456 | tf_op jit(solution)/shard_map/sjch,jhd->sjcd/dot_general | solution.py:167
  410.1 5.7 %copy.96 = bf16[8,2,54,1344]{3,1,2,0:T(2,128)(2,1)} copy(bf16[8,2,54,1344]{3,2,0,1:T(8,128)(2,1)} %fusion.20) | data formatting | bytes 4644864 | tf_op jit(solution)/shard_map/convert_element_type | solution.py:173
  415.8 5.6 %all-to-all-start.1 = ((bf16[8,2,54,1344]{3,1,2,0:T(2,128)(2,1)}), bf16[8,2,54,1344]{3,1,2,0:T(2,128)(2,1)}, u32[]{:S(2)}, u32[]{:S(2)}) async-start(bf16[8,2,54,1344]{3,1,2,0:T(2,128)(2,1)} %copy.96), calls=%async_computation.1 | async-start | bytes 4866048 | tf_op jit(solution)/shard_map/all_to_all | solution.py:174
  422.2 4.4 fusion.38
  427.0 1.0 fusion.37
  427.9 1.6 fusion.42
  429.6 4.6 convolution_add_fusion
  434.2 2.5 fusion.14
  436.9 16.7 %reduce-scatter.2.cloned.1.call-done = bf16[128,1344]{0,1:T(8,128)(2,1)} async-done(((bf16[128,2688]{0,1:T(8,128)(2,1)}), bf16[128,1344]{0,1:T(8,128)(2,1)}) %reduce-scatter.2.cloned.1.call-update) | async-done | bytes 344080 | tf_op jit(solution)/shard_map/reduce_scatter | solution.py:164
  453.5 23.2 %all-to-all-done.1 = bf16[8,2,54,1344]{3,1,2,0:T(2,128)(2,1)} async-done(((bf16[8,2,54,1344]{3,1,2,0:T(2,128)(2,1)}), bf16[8,2,54,1344]{3,1,2,0:T(2,128)(2,1)}, u32[]{:S(2)}, u32[]{:S(2)}) %all-to-all-start.1) | async-done | bytes 2322464 | tf_op jit(solution)/shard_map/all_to_all | solution.py:174
  476.8 3.5 copy.97
  480.3 4.4 reshape.65
  484.7 3.0 convolution_convert_fusion.1
  487.8 1.6 collective-permute-done
  489.4 0.7 copy.171
  (63 shorter events, 3.9 us)
Async XLA Ops:
  7.2 420.8 %copy-start = (bf16[2688,256]{1,0:T(8,128)(2,1)S(1)}, bf16[2688,256]{1,0:T(8,128)(2,1)}, u32[]{:S(2)}) copy-start(bf16[2688,256]{1,0:T(8,128)(2,1)} %param.25) | copy-start | bytes 4128772
  10.9 0.5 copy-start.7
  10.9 0.5 copy-start.9
  10.9 0.5 copy-start.11
  11.0 0.6 copy-start.13
  51.9 7.5 %copy-start.5 = (f32[2688]{0:T(1024)S(1)}, f32[2688]{0:T(1024)}, u32[]{:S(2)}) copy-start(f32[2688]{0:T(1024)} %param.15) | copy-start | bytes 32260
  52.0 63.0 %all-to-all-start = ((bf16[8,2,54,1344]{3,1,2,0:T(2,128)(2,1)}), bf16[8,2,54,1344]{3,1,2,0:T(2,128)(2,1)}, u32[]{:S(2)}, u32[]{:S(2)}) async-start(bf16[8,2,54,1344]{3,1,2,0:T(2,128)(2,1)} %copy.87), calls=%async_computation | async-start | bytes 4866048 | tf_op jit(solution)/shard_map/all_to_all | solution.py:144
  59.4 202.8 %all-gather.3.cloned.1.call-start = ((), (), s32[]{:S(2)}) async-start(), calls=%async_computation.3 | async-start | bytes 16515072 | tf_op jit(solution)/shard_map/all_gather | solution.py:151
  127.8 262.2 %all-gather.5.cloned.1.call-start = ((), (), s32[]{:S(2)}) async-start(), calls=%async_computation.4 | async-start | bytes 11403264 | tf_op jit(solution)/shard_map/all_gather | solution.py:169
  278.9 10.1 %copy-start.1 = (bf16[8,2,54,928]{3,2,0,1:T(8,128)(2,1)S(1)}, bf16[8,2,54,928]{3,2,0,1:T(8,128)(2,1)}, u32[]{:S(2)}) copy-start(bf16[8,2,54,928]{3,2,0,1:T(8,128)(2,1)} %convert_bitcast_fusion.1) | copy-start | bytes 4810756
  415.8 6.0 %copy-start.3 = (bf16[1,128,1024]{2,1,0:T(8,128)(2,1)S(1)}, bf16[1,128,1024]{2,1,0:T(8,128)(2,1)}, u32[]{:S(2)}) copy-start(bf16[1,128,1024]{2,1,0:T(8,128)(2,1)} %param.20) | copy-start | bytes 786436
  415.8 6.1 %copy-start.4 = (bf16[1,128,256]{2,1,0:T(8,128)(2,1)S(1)}, bf16[1,128,256]{2,1,0:T(8,128)(2,1)}, u32[]{:S(2)}) copy-start(bf16[1,128,256]{2,1,0:T(8,128)(2,1)} %param.21) | copy-start | bytes 196612
  415.8 6.4 %copy-start.2 = (bf16[1,128,2688]{2,1,0:T(8,128)(2,1)S(1)}, bf16[1,128,2688]{2,1,0:T(8,128)(2,1)}, u32[]{:S(2)}) copy-start(bf16[1,128,2688]{2,1,0:T(8,128)(2,1)} %param.23) | copy-start | bytes 2064388
  415.8 61.0 %all-to-all-start.1 = ((bf16[8,2,54,1344]{3,1,2,0:T(2,128)(2,1)}), bf16[8,2,54,1344]{3,1,2,0:T(2,128)(2,1)}, u32[]{:S(2)}, u32[]{:S(2)}) async-start(bf16[8,2,54,1344]{3,1,2,0:T(2,128)(2,1)} %copy.96), calls=%async_computation.1 | async-start | bytes 4866048 | tf_op jit(solution)/shard_map/all_to_all | solution.py:174
  421.4 32.1 %reduce-scatter.2.cloned.1.call-start = ((), (), s32[]{:S(2)}) async-start(), calls=%async_computation.5 | async-start | bytes 1032192 | tf_op jit(solution)/shard_map/reduce_scatter | solution.py:164
  421.8 4.8 copy-start.15
  434.2 2.6 copy-start.6
  453.5 34.3 %collective-permute-start.1 = (bf16[128,1344]{0,1:T(8,128)(2,1)}, bf16[128,1344]{0,1:T(8,128)(2,1)S(1)}, u32[]{:S(2)}, u32[]{:S(2)}) collective-permute-start(bf16[128,1344]{0,1:T(8,128)(2,1)} %reduce-scatter.2.cloned.1.call-done), channel_id=1, source_target_pairs={{0,16},{16,0},{1,17},{17,1},{2,18},{18,2},{3,19},{19,3},{4,20},{20... | collective-permute-start | bytes 1032200 | tf_op jit(solution)/shard_map/ppermute | solution.py:21
  480.3 4.4 copy-start.8
  480.3 4.4 copy-start.10
  480.3 4.4 copy-start.12
  480.3 4.4 copy-start.14
  487.7 1.7 collective-permute-start
Sparse Core Ops, SparseCore 0:
  127.9 134.2 all-gather.2
  294.8 95.1 all-gather.4
  436.9 16.5 reduce-scatter.1
where the time goes:
time: 499 us; the launch traced here: 497 us
  waiting for transfers between devices  322 us (65%)
  local copies, waits for them, and re-layouts  74 us (15%)
  matrix products  62.6 us (13%)
  between operations  14.1 us (3%)
  starting transfers between devices  13.5 us (3%)
  other arithmetic  6.66 us (1%)
    all_gather x1, waiting for transfers between devices, on_device(): piece = lax.all_gather(scaled, 'dp', axis=3, tiled=True)  129 us
    all_gather x1, waiting for transfers between devices, on_device(): lax.all_gather(hidden, 'dp', axis=3, tiled=True)  95.3 us
    all_to_all x1, waiting for transfers between devices, on_device(): lax.all_to_all(outgoing, 'expert', split_axis=0, concat_axis=0, tiled=True)  55.4 us
    reshape x2, local copies, waits for them, and re-layouts, on_device(): outgoing = outgoing.reshape(columns, local_experts, capacity, feature_share)  37 us
    all_to_all x1, waiting for transfers between devices, on_device(): lax.all_to_all(expert_rows, 'expert', split_axis=0, concat_axis=0, tiled=...  23.2 us
    dot_general x2, matrix products, block_product(): jnp.einsum('sjcw,jwh->sjch', block_rows, weight_rows, preferred_element_t...  21.2 us
    dot_general x1, matrix products, on_device(): jnp.einsum('sjch,jhd->sjcd', lax.all_gather(hidden, 'dp', axis=3, tiled=T...  20.2 us
    reduce_scatter x1, waiting for transfers between devices, on_device(): lax.psum_scatter(grad_term.astype(jnp.bfloat16), 'dp', scatter_dimension=...  16.7 us
  transfers between devices with their start and end apart: 7, of which 6 were waited for; matrix products, arithmetic and copies ran while one was open for 5% of the time, Pallas kernels for 0%

commit v1 on v0

--- a/solution.py
+++ b/solution.py
@@ -9,6 +9,20 @@
 HEAD_DIM = 128
 TOPK = 6
 NORM_EPSILON = 1e-05
+
+
+def find_hubs(packet, axis_k, t0):
+    z_new = packet.shape
+    now = packet.reshape(*z_new[:axis_k], t0, z_new[axis_k] // t0, *z_new[axis_k + 1 :])
+    q_next = jnp.moveaxis(now, axis_k, 0)
+    return q_next
+
+
+def solve_results_up(u_in, ndim_at):
+    block_last = list(u_in.shape[1:])
+    block_last[ndim_at] *= u_in.shape[0]
+    seen_now = jnp.moveaxis(u_in, 0, ndim_at).reshape(block_last)
+    return seen_now
 
 
 def partner(block, axis, distance):
@@ -141,7 +155,17 @@
         "ts,tw->sw", spread, token_rows, preferred_element_type=jnp.float32
     ).astype(jnp.bfloat16)
     outgoing = outgoing.reshape(columns, local_experts, capacity, feature_share)
-    arrived = lax.all_to_all(outgoing, "expert", split_axis=0, concat_axis=0, tiled=True)
+    met_up = lax.axis_size("expert")
+    frame_out = lax.axis_index("expert")
+    newest, p_next = (met_up, frame_out)
+    wide_out = find_hubs(outgoing, 0, newest)
+    out_arr = wide_out
+    for kk in range(1, newest):
+        val, extra = ((p_next + kk) % newest, (p_next - kk) % newest)
+        latest = lax.dynamic_index_in_dim(wide_out, val, 0)
+        x_now = lax.ppermute(latest, "expert", [(d, (d + kk) % newest) for d in range(newest)])
+        out_arr = lax.dynamic_update_slice_in_dim(out_arr, x_now, extra, axis=0)
+    arrived = solve_results_up(out_arr, 0)
     arrived_wide = arrived.astype(jnp.float32)
     start_up = jnp.zeros((columns, local_experts, capacity, hidden_share), jnp.float32)
     squares = lax.psum(jnp.sum(jnp.square(arrived_wide), axis=3), "dp")

time: 499 us -> 474 us (0.950)
  waiting for transfers between devices: 322 us -> 300 us
  local copies, waits for them, and re-layouts: 74 us -> 61.5 us
  starting transfers between devices: 13.5 us -> 22.7 us
    all_to_all x1 -> x0, waiting for transfers between devices: 55.4 us -> none  [on_device(): lax.all_to_all(outgoing, 'expert', split_axis=0, concat_axis=0, tiled=True)]
    reshape x2 -> x1, local copies, waits for them, and re-layouts: 37 us -> 4.2 us  [solve_results_up(): seen_now = jnp.moveaxis(u_in, 0, ndim_at).reshape(block_last)]
    all_gather x1, waiting for transfers between devices: 129 us -> 147 us  [on_device(): piece = lax.all_gather(scaled, 'dp', axis=3, tiled=True)]
    ppermute x0 -> x7, waiting for transfers between devices: none -> 16.6 us  [on_device(): lax.ppermute(latest, 'expert', [(d, (d + kk) % newest) for d in range(new...]
    ppermute x0 -> x7, starting transfers between devices: none -> 16.6 us  [on_device(): lax.ppermute(latest, 'expert', [(d, (d + kk) % newest) for d in range(new...]
    dynamic_update_slice x0 -> x7, local copies, waits for them, and re-layouts: none -> 10.1 us  [on_device(): out_arr = lax.dynamic_update_slice_in_dim(out_arr, x_now, extra, axis=0)]
    all_to_all x1 -> x0, starting transfers between devices: 7.44 us -> none  [on_device(): lax.all_to_all(outgoing, 'expert', split_axis=0, concat_axis=0, tiled=True)]
  transfers between devices with their start and end apart: 7 -> 13, of which waited for: 6 -> 6; matrix products, arithmetic and copies ran while one was open for 5% -> 8% of each run, Pallas kernels for 0% -> 0%
where the time goes in v1:
time: 474 us; the launch traced here: 473 us
  waiting for transfers between devices  300 us (63%)
  matrix products  62.7 us (13%)
  local copies, waits for them, and re-layouts  61.5 us (13%)
  starting transfers between devices  22.7 us (5%)
  between operations  14.2 us (3%)
  other arithmetic  6.74 us (1%)
  blocking collectives  5 us (1%)
    all_gather x1, waiting for transfers between devices, on_device(): piece = lax.all_gather(scaled, 'dp', axis=3, tiled=True)  147 us
    all_gather x1, waiting for transfers between devices, on_device(): lax.all_gather(hidden, 'dp', axis=3, tiled=True)  95.3 us
    all_to_all x1, waiting for transfers between devices, on_device(): lax.all_to_all(expert_rows, 'expert', split_axis=0, concat_axis=0, tiled=...  23.2 us
    dot_general x2, matrix products, block_product(): jnp.einsum('sjcw,jwh->sjch', block_rows, weight_rows, preferred_element_t...  21.2 us
    dot_general x1, matrix products, on_device(): jnp.einsum('sjch,jhd->sjcd', lax.all_gather(hidden, 'dp', axis=3, tiled=T...  20.2 us
    reduce_scatter x1, waiting for transfers between devices, on_device(): lax.psum_scatter(grad_term.astype(jnp.bfloat16), 'dp', scatter_dimension=...  16.7 us
    ppermute x7, waiting for transfers between devices, on_device(): lax.ppermute(latest, 'expert', [(d, (d + kk) % newest) for d in range(new...  16.6 us
    ppermute x7, starting transfers between devices, on_device(): lax.ppermute(latest, 'expert', [(d, (d + kk) % newest) for d in range(new...  16.6 us
  transfers between devices with their start and end apart: 13, of which 6 were waited for; matrix products, arithmetic and copies ran while one was open for 8% of the time, Pallas kernels for 0%

profile of v1, /device:TPU:0, one launch (start us, length us, event | category | flops | bytes accessed | tf_op | source)
XLA Modules:
  0.0 473.2 jit_solution(16640605087813781126)
XLA Ops:
  11.6 3.5 convolution_convert_fusion
  15.1 4.4 copy.123
  19.5 4.2 reshape_reshape.3
  23.7 2.4 constant_dynamic-slice_fusion
  26.1 3.0 collective-permute-start
  30.7 2.5 collective-permute-start.2
  34.4 2.6 collective-permute-start.4
  37.1 4.2 reshape.93
  44.4 4.3 collective-permute-start.6
  50.4 16.6 %collective-permute-done.2 = bf16[1,1,2,54,1344]{4,3,2,1,0:T(8,128)(2,1)} collective-permute-done((bf16[1,1,2,54,1344]{4,3,2,1,0:T(8,128)(2,1)S(1)}, bf16[1,1,2,54,1344]{4,3,2,1,0:T(8,128)(2,1)}, u32[]{:S(2)}, u32[]{:S(2)}) %collective-permute-start.2) | collective-permute-done | bytes 290336 | tf_op jit(solution)/shard_map/ppermute | solution.py:166
  68.8 1.7 bitcast_dynamic-update-slice_fusion.3
  70.5 1.7 bitcast_dynamic-update-slice_fusion.2
  73.7 4.0 fusion.13
  77.7 8.3 %copy.132 = bf16[8,2,54,1344]{2,0,1,3:T(8,128)(2,1)} copy(bf16[8,2,54,1344]{3,2,1,0:T(8,128)(2,1)} %get-tuple-element.11) | data formatting | bytes 4644864 | tf_op jit(solution)/shard_map/convert_element_type | solution.py:173
  86.0 5.0 %psum.7 = f32[8,2,54]{2,0,1:T(8,128)S(1)} all-reduce(f32[8,2,54]{2,0,1:T(8,128)S(1)} %copy.135), channel_id=1, replica_groups=mesh['segment'=2,'expert'=8,'dp'=2] {'dp'}, use_global_device_ids=true, to_apply=%region_5.6 | all-reduce | flops 864 | bytes 6912 | tf_op jit(solution)/shard_map/psum | solution.py:171
  91.0 147.0 %all-gather.3.cloned.1.call-done = bf16[8,2,54,2688]{2,0,1,3:T(8,128)(2,1)} async-done(((bf16[8,2,54,1344]{2,0,1,3:T(8,128)(2,1)}), bf16[8,2,54,2688]{2,0,1,3:T(8,128)(2,1)}) %all-gather.3.cloned.1.call-update) | async-done | bytes 4644880 | tf_op jit(solution)/shard_map/all_gather | solution.py:175
  238.0 5.5 %fusion.112 = (bf16[8,2,54,1344]{2,0,1,3:T(8,128)(2,1)S(1)}, bf16[8,2,54,1344]{2,0,1,3:T(8,128)(2,1)S(1)}) fusion(bf16[8,2,54,2688]{2,0,1,3:T(8,128)(2,1)} %all-gather.3.cloned.1.call-done), kind=kLoop, calls=%fused_computation.146 | loop fusion | bytes 9289728 | tf_op jit(solution)/shard_map/slice | solution.py:180
  243.5 11.1 %convert_bitcast_fusion.1 = bf16[8,2,54,928]{3,2,0,1:T(8,128)(2,1)} fusion(bf16[2,2688,928]{1,2,0:T(8,128)(2,1)} %param.18, bf16[8,2,54,1344]{2,0,1,3:T(8,128)(2,1)S(1)} %get-tuple-element.8), kind=kOutput, calls=%fused_computation.25 | convolution fusion | flops 2156018688 | bytes 9152512 | tf_op jit(solution)/shard_map/sjcw,jwh->sjch/dot_general | solution.py:98
  254.7 10.0 %convert_bitcast_fusion = bf16[8,2,54,928]{3,2,0,1:T(8,128)(2,1)S(1)} fusion(bf16[2,2688,928]{1,2,0:T(8,128)(2,1)} %param.18, bf16[8,2,54,1344]{2,0,1,3:T(8,128)(2,1)S(1)} %get-tuple-element.9), kind=kOutput, calls=%fused_computation.24 | convolution fusion | flops 2156018688 | bytes 9152512 | tf_op jit(solution)/shard_map/sjcw,jwh->sjch/dot_general | solution.py:98
  265.5 4.9 %copy.136 = bf16[8,2,54,928]{2,0,1,3:T(8,128)(2,1)} copy(bf16[8,2,54,928]{3,2,0,1:T(8,128)(2,1)S(1)} %multiply_convert_fusion) | data formatting | bytes 3207168 | tf_op jit(solution)/shard_map/convert_element_type | solution.py:184
  270.5 95.3 %all-gather.5.cloned.1.call-done = bf16[8,2,54,1856]{2,0,1,3:T(8,128)(2,1)} async-done(((bf16[8,2,54,928]{2,0,1,3:T(8,128)(2,1)}), bf16[8,2,54,1856]{2,0,1,3:T(8,128)(2,1)}) %all-gather.5.cloned.1.call-update) | async-done | bytes 3207184 | tf_op jit(solution)/shard_map/all_gather | solution.py:193
  365.7 20.2 %fusion.20 = bf16[8,2,54,1344]{3,2,0,1:T(8,128)(2,1)} fusion(bf16[2,1856,1344]{1,2,0:T(8,128)(2,1)} %param.19, bf16[8,2,54,1856]{2,0,1,3:T(8,128)(2,1)} %all-gather.5.cloned.1.call-done), kind=kOutput, calls=%fused_computation.22 | convolution fusion | flops 4311595008 | bytes 15507456 | tf_op jit(solution)/shard_map/sjch,jhd->sjcd/dot_general | solution.py:191
  385.9 5.7 %copy.138 = bf16[8,2,54,1344]{3,1,2,0:T(2,128)(2,1)} copy(bf16[8,2,54,1344]{3,2,0,1:T(8,128)(2,1)} %fusion.20) | data formatting | bytes 4644864 | tf_op jit(solution)/shard_map/convert_element_type | solution.py:197
  391.6 5.6 %all-to-all-start = ((bf16[8,2,54,1344]{3,1,2,0:T(2,128)(2,1)}), bf16[8,2,54,1344]{3,1,2,0:T(2,128)(2,1)}, u32[]{:S(2)}, u32[]{:S(2)}) async-start(bf16[8,2,54,1344]{3,1,2,0:T(2,128)(2,1)} %copy.138), calls=%async_computation | async-start | bytes 4866048 | tf_op jit(solution)/shard_map/all_to_all | solution.py:198
  398.0 4.5 fusion.38
  405.4 4.6 convolution_add_fusion
  410.1 2.5 fusion.14
  412.7 16.7 %reduce-scatter.2.cloned.1.call-done = bf16[128,1344]{0,1:T(8,128)(2,1)} async-done(((bf16[128,2688]{0,1:T(8,128)(2,1)}), bf16[128,1344]{0,1:T(8,128)(2,1)}) %reduce-scatter.2.cloned.1.call-update) | async-done | bytes 344080 | tf_op jit(solution)/shard_map/reduce_scatter | solution.py:188
  429.4 23.2 %all-to-all-done = bf16[8,2,54,1344]{3,1,2,0:T(2,128)(2,1)} async-done(((bf16[8,2,54,1344]{3,1,2,0:T(2,128)(2,1)}), bf16[8,2,54,1344]{3,1,2,0:T(2,128)(2,1)}, u32[]{:S(2)}, u32[]{:S(2)}) %all-to-all-start) | async-done | bytes 2322464 | tf_op jit(solution)/shard_map/all_to_all | solution.py:198
  452.6 3.5 copy.139
  456.1 4.4 reshape.101
  460.5 3.0 convolution_convert_fusion.1
  (84 shorter events, 22.9 us)
Async XLA Ops:
  7.2 396.6 %copy-start = (bf16[2688,256]{1,0:T(8,128)(2,1)S(1)}, bf16[2688,256]{1,0:T(8,128)(2,1)}, u32[]{:S(2)}) copy-start(bf16[2688,256]{1,0:T(8,128)(2,1)} %param.25) | copy-start | bytes 4128772
  7.2 230.8 %all-gather.3.cloned.1.call-start = ((), (), s32[]{:S(2)}) async-start(), calls=%async_computation.2 | async-start | bytes 16515072 | tf_op jit(solution)/shard_map/all_gather | solution.py:175
  11.0 0.5 copy-start.7
  11.0 0.5 copy-start.9
  11.1 0.5 copy-start.11
  11.1 0.6 copy-start.13
  26.1 15.3 %collective-permute-start = (bf16[1,1,2,54,1344]{4,3,2,1,0:T(8,128)(2,1)}, bf16[1,1,2,54,1344]{4,3,2,1,0:T(8,128)(2,1)}, u32[]{:S(2)}, u32[]{:S(2)}) collective-permute-start(bf16[1,1,2,54,1344]{4,3,2,1,0:T(8,128)(2,1)} %get-tuple-element.18), channel_id=1, source_target_pairs={{0,2},{2,4},{4,6},{6,8},{8,10},{10,12},{12,14},{14,0},{1,3},{3,5},... | collective-permute-start | bytes 870920 | tf_op jit(solution)/shard_map/ppermute | solution.py:166
  29.1 15.3 %collective-permute-start.1 = (bf16[1,1,2,54,1344]{4,3,2,1,0:T(8,128)(2,1)S(1)}, bf16[1,1,2,54,1344]{4,3,2,1,0:T(8,128)(2,1)}, u32[]{:S(2)}, u32[]{:S(2)}) collective-permute-start(bf16[1,1,2,54,1344]{4,3,2,1,0:T(8,128)(2,1)S(1)} %get-tuple-element.17), channel_id=1, source_target_pairs={{0,4},{2,6},{4,8},{6,10},{8,12},{10,14},{12,0},{14,2},{1,5},{3,7},... | collective-permute-start | bytes 870920 | tf_op jit(solution)/shard_map/ppermute | solution.py:166
  30.7 36.4 %collective-permute-start.2 = (bf16[1,1,2,54,1344]{4,3,2,1,0:T(8,128)(2,1)S(1)}, bf16[1,1,2,54,1344]{4,3,2,1,0:T(8,128)(2,1)}, u32[]{:S(2)}, u32[]{:S(2)}) collective-permute-start(bf16[1,1,2,54,1344]{4,3,2,1,0:T(8,128)(2,1)S(1)} %get-tuple-element.16), channel_id=1, source_target_pairs={{0,6},{2,8},{4,10},{6,12},{8,14},{10,0},{12,2},{14,4},{1,7},{3,9},... | collective-permute-start | bytes 870920 | tf_op jit(solution)/shard_map/ppermute | solution.py:166
  33.2 35.6 %collective-permute-start.3 = (bf16[1,1,2,54,1344]{4,3,2,1,0:T(8,128)(2,1)S(1)}, bf16[1,1,2,54,1344]{4,3,2,1,0:T(8,128)(2,1)}, u32[]{:S(2)}, u32[]{:S(2)}) collective-permute-start(bf16[1,1,2,54,1344]{4,3,2,1,0:T(8,128)(2,1)S(1)} %get-tuple-element.15), channel_id=1, source_target_pairs={{0,8},{2,10},{4,12},{6,14},{8,0},{10,2},{12,4},{14,6},{1,9},{3,11}... | collective-permute-start | bytes 870920 | tf_op jit(solution)/shard_map/ppermute | solution.py:166
  34.4 36.1 %collective-permute-start.4 = (bf16[1,1,2,54,1344]{4,3,2,1,0:T(8,128)(2,1)S(1)}, bf16[1,1,2,54,1344]{4,3,2,1,0:T(8,128)(2,1)}, u32[]{:S(2)}, u32[]{:S(2)}) collective-permute-start(bf16[1,1,2,54,1344]{4,3,2,1,0:T(8,128)(2,1)S(1)} %get-tuple-element.14), channel_id=1, source_target_pairs={{0,10},{2,12},{4,14},{6,0},{8,2},{10,4},{12,6},{14,8},{1,11},{3,13... | collective-permute-start | bytes 870920 | tf_op jit(solution)/shard_map/ppermute | solution.py:166
  37.1 4.2 copy-start.5
  41.4 30.9 %collective-permute-start.5 = (bf16[1,1,2,54,1344]{4,3,2,1,0:T(8,128)(2,1)S(1)}, bf16[1,1,2,54,1344]{4,3,2,1,0:T(8,128)(2,1)S(1)}, u32[]{:S(2)}, u32[]{:S(2)}) collective-permute-start(bf16[1,1,2,54,1344]{4,3,2,1,0:T(8,128)(2,1)S(1)} %get-tuple-element.13), channel_id=1, source_target_pairs={{0,12},{2,14},{4,0},{6,2},{8,4},{10,6},{12,8},{14,10},{1,13},{3,15... | collective-permute-start | bytes 870920 | tf_op jit(solution)/shard_map/ppermute | solution.py:166
  44.4 28.6 %collective-permute-start.6 = (bf16[1,1,2,54,1344]{4,3,2,1,0:T(8,128)(2,1)S(1)}, bf16[1,1,2,54,1344]{4,3,2,1,0:T(8,128)(2,1)S(1)}, u32[]{:S(2)}, u32[]{:S(2)}) collective-permute-start(bf16[1,1,2,54,1344]{4,3,2,1,0:T(8,128)(2,1)S(1)} %get-tuple-element.12), channel_id=1, source_target_pairs={{0,14},{2,0},{4,2},{6,4},{8,6},{10,8},{12,10},{14,12},{1,15},{3,1}... | collective-permute-start | bytes 870920 | tf_op jit(solution)/shard_map/ppermute | solution.py:166
  86.0 279.8 %all-gather.5.cloned.1.call-start = ((), (), s32[]{:S(2)}) async-start(), calls=%async_computation.3 | async-start | bytes 11403264 | tf_op jit(solution)/shard_map/all_gather | solution.py:193
  254.7 10.1 %copy-start.1 = (bf16[8,2,54,928]{3,2,0,1:T(8,128)(2,1)S(1)}, bf16[8,2,54,928]{3,2,0,1:T(8,128)(2,1)}, u32[]{:S(2)}) copy-start(bf16[8,2,54,928]{3,2,0,1:T(8,128)(2,1)} %convert_bitcast_fusion.1) | copy-start | bytes 4810756
  391.6 6.0 %copy-start.3 = (bf16[1,128,1024]{2,1,0:T(8,128)(2,1)S(1)}, bf16[1,128,1024]{2,1,0:T(8,128)(2,1)}, u32[]{:S(2)}) copy-start(bf16[1,128,1024]{2,1,0:T(8,128)(2,1)} %param.20) | copy-start | bytes 786436
  391.6 6.1 %copy-start.4 = (bf16[1,128,256]{2,1,0:T(8,128)(2,1)S(1)}, bf16[1,128,256]{2,1,0:T(8,128)(2,1)}, u32[]{:S(2)}) copy-start(bf16[1,128,256]{2,1,0:T(8,128)(2,1)} %param.21) | copy-start | bytes 196612
  391.6 6.4 %copy-start.2 = (bf16[1,128,2688]{2,1,0:T(8,128)(2,1)S(1)}, bf16[1,128,2688]{2,1,0:T(8,128)(2,1)}, u32[]{:S(2)}) copy-start(bf16[1,128,2688]{2,1,0:T(8,128)(2,1)} %param.23) | copy-start | bytes 2064388
  391.6 61.0 %all-to-all-start = ((bf16[8,2,54,1344]{3,1,2,0:T(2,128)(2,1)}), bf16[8,2,54,1344]{3,1,2,0:T(2,128)(2,1)}, u32[]{:S(2)}, u32[]{:S(2)}) async-start(bf16[8,2,54,1344]{3,1,2,0:T(2,128)(2,1)} %copy.138), calls=%async_computation | async-start | bytes 4866048 | tf_op jit(solution)/shard_map/all_to_all | solution.py:198
  397.2 32.2 %reduce-scatter.2.cloned.1.call-start = ((), (), s32[]{:S(2)}) async-start(), calls=%async_computation.4 | async-start | bytes 1032192 | tf_op jit(solution)/shard_map/reduce_scatter | solution.py:188
  398.0 4.5 copy-start.15
  410.1 2.6 copy-start.6
  429.4 34.2 %collective-permute-start.8 = (bf16[128,1344]{0,1:T(8,128)(2,1)}, bf16[128,1344]{0,1:T(8,128)(2,1)S(1)}, u32[]{:S(2)}, u32[]{:S(2)}) collective-permute-start(bf16[128,1344]{0,1:T(8,128)(2,1)} %reduce-scatter.2.cloned.1.call-done), channel_id=1, source_target_pairs={{0,16},{16,0},{1,17},{17,1},{2,18},{18,2},{3,19},{19,3},{4,20},{20... | collective-permute-start | bytes 1032200 | tf_op jit(solution)/shard_map/ppermute | solution.py:35
  456.1 4.4 copy-start.8
  456.1 4.4 copy-start.10
  456.1 4.4 copy-start.12
  456.1 4.4 copy-start.14
  463.5 1.7 collective-permute-start.7
Sparse Core Ops, SparseCore 0:
  86.1 151.8 all-gather.2
  270.6 95.1 all-gather.4
  412.8 16.5 reduce-scatter.1
